TPU v7x, 32 devices: a whole 2x2x4 slice. The times are simulated.
32 devices in a mesh: groups: 2 (over x), seq: 4 (over y, core), chan: 4 (over z).
Axes of the slice: x: 2, y: 2, z: 4, core: 2. Of those that a mesh axis runs over, the one named last changes fastest.
Arguments:
- dna_act: bfloat16 [6, 2048, 1280], P('groups', 'seq', 'chan'), parts along dimension 0, may hold values from -5 to 5
- conv_weight: bfloat16 [5, 1280, 1536], P(None, 'chan'), may hold values from -0.078125 to 0.078125
- head_weight: bfloat16 [7611, 1536], P(None, 'chan'), may hold values from -0.078125 to 0.078125
- track_ids: int32 [1024], P('groups'), parts along dimension 0, may hold values from 0 to 7610, as said below
- bin_mask: int32 [6, 1024], P('groups', ('seq', 'chan')), parts along dimension 0, may hold values 0 or 1
- counts: int32 [6, 1024, 512], P('groups', ('seq', 'chan')), parts along dimension 0, may hold values from 0 to 3
Outputs:
- grad_input: bfloat16 [6, 2048, 1280], P('groups', 'seq', 'chan'), parts along dimension 0
- grad_conv: float32 [10, 1280, 1536], P('groups', 'chan', 'seq'), parts along dimension 0
- grad_tracks: float32 [1024, 1536], P(('groups', 'seq'), 'chan'), parts along dimension 0
There are 2 independent parts, one for each index of `groups`. A program takes and returns all parts, laid end to end along the dimension named above; an argument that names none is the same for every part. Nothing has to cross between parts.
Inputs may be any that keep to these rules, and one draw needn't show every extreme that they name: `track_ids`: the 512 track numbers are distinct.
All inputs are finite; a program needn't handle non-finite values. No bound on the sum of `bin_mask` on one device may be relied on, other than what follows from the above.
Results may differ from a plain program's by a relative error of at most 0.011.
Values may be sent and summed in bfloat16 or wider, within the bound.
No kernel may reach another device: no remote copies, remote signals or barrier semaphores. Data moves between devices by JAX's collectives and lax.ppermute only.
A program may use at most 128 MiB of HBM per device.

v0:
```python
import jax
import jax.numpy as jnp
from jax import lax
from jax.sharding import PartitionSpec as P

KSIZE = 5


def padded_2(cells, sides, width):
    for axis, dim in sides:
        count = lax.axis_size(axis)
        ends = count - 1
        head = lax.slice_in_dim(cells, 0, width, axis=dim)
        tail = lax.slice_in_dim(cells, cells.shape[dim] - width, cells.shape[dim], axis=dim)
        cells = jnp.concatenate(
            [
                lax.ppermute(tail, axis, [(i, (i + 1) % count) for i in range(ends)]),
                cells,
                lax.ppermute(head, axis, [((i + 1) % count, i) for i in range(ends)]),
            ],
            axis=dim,
        )
    return cells


def exact_gelu(values):
    return jax.nn.gelu(values, approximate=False)


def local(dna_act, conv_weight, head_weight, track_ids, bin_mask, counts):
    seq_count, positions, channels = dna_act.shape
    out_width = conv_weight.shape[2]
    gelu_out, gelu_back = jax.vjp(exact_gelu, dna_act.astype(jnp.float32))
    activated = gelu_out.astype(jnp.bfloat16)
    padded = padded_2(activated, (("seq", 1),), 2)
    windows = jnp.concatenate(
        [padded[:, offset : offset + positions] for offset in range(KSIZE)], axis=2
    )
    flat_weight = conv_weight.reshape(KSIZE * channels, out_width)
    conv_part = jnp.einsum("stj,jo->sto", windows, flat_weight, preferred_element_type=jnp.float32)
    pooled_part = conv_part.reshape(seq_count, positions // 2, 2, out_width).sum(axis=2) * 0.5
    bin_rows = lax.psum_scatter(
        pooled_part.astype(jnp.bfloat16), "chan", scatter_dimension=1, tiled=True
    )
    local_rows = jnp.take(head_weight, track_ids, axis=0)
    chosen = lax.all_gather(local_rows, "chan", axis=1, tiled=True)
    logits = jnp.einsum("snd,md->snm", bin_rows, chosen, preferred_element_type=jnp.float32)
    mask_column = bin_mask.astype(jnp.float32)[:, :, None]
    grad_logit = (mask_column * (jnp.exp(logits) - counts.astype(jnp.float32))).astype(jnp.bfloat16)
    grad_bins = jnp.einsum(
        "snm,md->snd", grad_logit, chosen, preferred_element_type=jnp.float32
    ).astype(jnp.bfloat16)
    slab_grad = lax.all_gather(grad_bins, "chan", axis=1, tiled=True)
    track_part = jnp.einsum("snm,snd->md", grad_logit, bin_rows, preferred_element_type=jnp.float32)
    track_summed = lax.psum_scatter(
        track_part.astype(jnp.bfloat16), "seq", scatter_dimension=0, tiled=True
    )
    grad_tracks = lax.psum_scatter(track_summed, "chan", scatter_dimension=1, tiled=True).astype(
        jnp.float32
    )
    rim_grad = padded_2(slab_grad, (("seq", 1),), 1)
    wide_grad = jnp.repeat(rim_grad, 2, axis=1) * 0.5
    projected = jnp.einsum(
        "sqo,jo->sqj", wide_grad, flat_weight, preferred_element_type=jnp.float32
    )
    projected = projected.reshape(seq_count, positions + 4, KSIZE, channels)
    grad_acts = projected[:, 4 : 4 + positions, 0]
    for offset in range(1, KSIZE):
        grad_acts = grad_acts + projected[:, 4 - offset : 4 - offset + positions, offset]
    grad_input = gelu_back(grad_acts)[0].astype(jnp.bfloat16)
    slab_upsampled = jnp.repeat(slab_grad, 2, axis=1) * 0.5
    flat_grad = jnp.einsum(
        "stj,sto->jo", windows, slab_upsampled, preferred_element_type=jnp.float32
    )
    grad_conv = lax.psum_scatter(
        flat_grad.reshape(KSIZE, channels, out_width).astype(jnp.bfloat16),
        "seq",
        scatter_dimension=2,
        tiled=True,
    ).astype(jnp.float32)
    return (grad_input, grad_conv, grad_tracks)


def solution(mesh):
    in_specs = (
        P("groups", "seq", "chan"),
        P(None, "chan", None),
        P(None, "chan"),
        P("groups"),
        P("groups", ("seq", "chan")),
        P("groups", ("seq", "chan"), None),
    )
    out_specs = (
        P("groups", "seq", "chan"),
        P("groups", "chan", "seq"),
        P(("groups", "seq"), "chan"),
    )
    return jax.shard_map(local, mesh=mesh, in_specs=in_specs, out_specs=out_specs, check_vma=False)
```

profile of v0, /device:TPU:0, one launch (start us, length us, event | category | flops | bytes accessed | tf_op | source)
XLA Modules:
  0.0 317.8 jit_solution(13602244970949401829)
XLA Ops:
  7.2 0.0 all-gather.3.cloned.1.call-start
  7.2 1.7 copy.17
  8.9 0.0 copy-start.3
  8.9 6.0 %fusion.12 = (bf16[3,512,320]{2,1,0:T(8,128)(2,1)S(1)}, f32[3,512,320]{2,1,0:T(8,128)}) fusion(bf16[3,512,320]{2,1,0:T(8,128)(2,1)S(1)} %copy.17), kind=kLoop, calls=%fused_computation.19 | loop fusion | flops 32440320 | bytes 3932160 | tf_op jit(solution)/shard_map/convert_element_type | solution.py:34
  15.0 2.4 collective-permute-start
  17.4 1.3 collective-permute-start.1
  18.7 0.0 copy-done.3
  18.7 5.2 %gather_fusion = bf16[512,384]{1,0:T(8,128)(2,1)S(1)} fusion(bf16[7611,384]{1,0:T(8,128)(2,1)} %param.8, s32[1024]{0:T(1024)S(1)} %pad_clamp_fusion), kind=kCustom, calls=%fused_computation | custom fusion | bytes 788480 | tf_op jit(solution)/shard_map/jit(_take)/gather | solution.py:45
  23.9 0.9 broadcast_select_fusion
  24.8 0.0 all-gather.3.cloned.1.call-update
  24.9 0.0 reduce-scatter.9.cloned.1.call-start
  24.9 0.0 collective-permute-done
  24.9 0.0 collective-permute-done.1
  24.9 3.4 %pad_maximum_fusion = (bf16[3,512,320]{2,1,0:T(8,128)(2,1)S(1)}, bf16[3,512,320]{2,1,0:T(8,128)(2,1)}, bf16[3,512,320]{2,1,0:T(8,128)(2,1)}, bf16[3,512,320]{2,1,0:T(8,128)(2,1)}) fusion(bf16[3,2,320]{2,1,0:T(2,128)(2,1)S(1)} %collective-permute-done.1, bf16[3,512,320]{2,1,0:T(8,128)(2,1)S(1)} %get-tuple-element.12, ...), kind=kLoop, calls=%fused_computation.71 | loop fusion | flops 7864320 | bytes 4922880 | tf_op jit(solution)/shard_map/concatenate | solution.py:15
  28.3 9.0 %concatenate.17 = bf16[3,512,1600]{2,1,0:T(8,128)(2,1)} concatenate(bf16[3,512,320]{2,1,0:T(8,128)(2,1)} %get-tuple-element.20, bf16[3,512,320]{2,1,0:T(8,128)(2,1)} %get-tuple-element.21, bf16[3,512,320]{2,1,0:T(8,128)(2,1)S(1)} %get-tuple-element.12, bf16[3,512,320]{2,1,0:T(8,128)(2,1)} %get-tuple-element.17, bf16[3,512,320]{2,1,0:T(8,128)(2,1)S(1)} %get-tuple-element.16), dimensions={2} | concatenate | bytes 9830400 | tf_op jit(solution)/shard_map/concatenate | solution.py:36
  37.3 11.0 %dot_general.24 = bf16[3,256,2,1600]{3,2,1,0:T(2,128)(2,1)} reshape(bf16[3,512,1600]{2,1,0:T(8,128)(2,1)} %concatenate.17) | data formatting | bytes 9830400 | tf_op jit(solution)/shard_map/stj,jo->sto/dot_general | solution.py:40
  48.3 12.4 %fusion.7 = f32[3,256,1536]{2,1,0:T(8,128)S(1)} fusion(bf16[1600,1536,1,1]{1,0,3,2:T(8,128)(2,1)} %bitcast.55, bf16[3,256,2,1600]{3,2,1,0:T(2,128)(2,1)} %dot_general.24), kind=kOutput, calls=%fused_computation.14 | convolution fusion | flops 7550926848 | bytes 14548992 | tf_op jit(solution)/shard_map/stj,jo->sto/dot_general | solution.py:40
  60.7 2.1 multiply_convert_fusion
  62.8 0.0 copy-start.4
  62.8 0.0 reduce-scatter.9.cloned.1.call-update
  62.8 0.0 reduce-scatter.11.cloned.1.call-start
  62.9 0.6 copy-done.4
  63.5 2.7 all-gather.3.cloned.1.call-done
  66.2 49.4 %reduce-scatter.9.cloned.1.call-done = bf16[3,64,1536]{2,1,0:T(8,128)(2,1)} async-done(((bf16[3,256,1536]{2,1,0:T(8,128)(2,1)}), bf16[3,64,1536]{2,1,0:T(8,128)(2,1)}) %reduce-scatter.9.cloned.1.call-update) | async-done | bytes 589840 | tf_op jit(solution)/shard_map/reduce_scatter | solution.py:42
  115.6 0.0 copy-done.2
  115.6 2.3 fusion.62
  117.9 0.0 copy-done.1
  117.9 1.8 fusion.6
  119.7 0.0 reduce-scatter.11.cloned.1.call-update
  119.7 0.0 all-gather.5.cloned.1.call-start
  119.8 2.7 convolution_convert_fusion
  122.5 0.0 all-gather.5.cloned.1.call-update
  122.5 0.2 reduce-scatter.15.cloned.1.call-start
  122.7 7.8 %copy.19 = bf16[1600,3,512]{2,0,1:T(8,128)(2,1)} copy(bf16[1600,3,512]{0,2,1:T(8,128)(2,1)} %bitcast.49) | data formatting | bytes 9830400 | tf_op jit(solution)/shard_map/stj,sto->jo/dot_general | solution.py:72
  130.5 16.8 %reduce-scatter.11.cloned.1.call-done = bf16[128,1536]{1,0:T(8,128)(2,1)} async-done(((bf16[512,1536]{1,0:T(8,128)(2,1)}), bf16[128,1536]{1,0:T(8,128)(2,1)}) %reduce-scatter.11.cloned.1.call-update) | async-done | bytes 393232 | tf_op jit(solution)/shard_map/reduce_scatter | solution.py:55
  147.3 1.9 copy.26
  149.2 0.0 reduce-scatter.15.cloned.1.call-update
  149.2 0.0 reduce-scatter.13.cloned.1.call-start
  149.3 50.0 %all-gather.5.cloned.1.call-done = bf16[3,256,1536]{2,1,0:T(8,128)(2,1)} async-done(((bf16[3,64,1536]{2,1,0:T(8,128)(2,1)}), bf16[3,256,1536]{2,1,0:T(8,128)(2,1)}) %all-gather.5.cloned.1.call-update) | async-done | bytes 2359312 | tf_op jit(solution)/shard_map/all_gather | solution.py:53
  199.3 1.9 broadcast_multiply_fusion
  201.2 4.0 %broadcast_in_dim.23 = bf16[3,256,2,1536]{3,2,1,0:T(2,128)(2,1)} broadcast(bf16[3,256,1536]{2,1,0:T(8,128)(2,1)S(1)} %broadcast_multiply_fusion), dimensions={0,1,3} | broadcast | bytes 7077888 | tf_op jit(solution)/shard_map/broadcast_in_dim | solution.py:71
  205.2 10.7 %reshape.44 = bf16[3,512,1536,1]{2,1,0,3:T(8,128)(2,1)} reshape(bf16[3,256,2,1536]{3,2,1,0:T(2,128)(2,1)} %broadcast_in_dim.23) | data formatting | bytes 9437184 | tf_op jit(solution)/shard_map/mul | solution.py:71
  215.9 12.5 %bitcast_convert_fusion = bf16[5,320,1536]{2,1,0:T(8,128)(2,1)} fusion(bf16[5,320,3,512]{3,1,0,2:T(8,128)(2,1)} %bitcast.52, bf16[3,512,1536,1]{2,1,0,3:T(8,128)(2,1)} %reshape.44), kind=kOutput, calls=%fused_computation.1 | convolution fusion | flops 7552204800 | bytes 14548992 | tf_op jit(solution)/shard_map/stj,sto->jo/dot_general | solution.py:72
  228.5 11.7 %copy.24 = bf16[5,320,1536]{1,0,2:T(8,128)(2,1)} copy(bf16[5,320,1536]{2,1,0:T(8,128)(2,1)} %bitcast_convert_fusion) | data formatting | bytes 9830400
  240.2 12.8 %reshape.49 = bf16[1536,1600]{1,0:T(8,128)(2,1)} reshape(bf16[1536,5,320]{2,1,0:T(8,128)(2,1)} %bitcast.50) | data formatting | bytes 9830400
  253.0 0.0 reduce-scatter.13.cloned.1.call-update
  253.0 1.0 fusion.66
  254.0 1.6 collective-permute-start.2
  255.5 1.3 collective-permute-start.3
  256.8 0.0 collective-permute-done.2
  256.9 3.2 collective-permute-done.3
  260.0 3.2 %maximum_multiply_fusion = bf16[3,258,1536]{2,1,0:T(8,128)(2,1)S(1)} fusion(bf16[3,1,1536]{2,1,0:T(2,128)(2,1)S(1)} %collective-permute-done.3, bf16[3,256,1536]{2,1,0:T(8,128)(2,1)} %all-gather.5.cloned.1.call-done, bf16[3,1,1536]{2,1,0:T(2,128)(2,1)S(1)} %collective-permute-done.2), kind=kLoop, calls=%fused_computation.18 | loop fusion | flops 9510912 | bytes 4755456 | tf_op jit(solution)/shard_map/mul | solution.py:62
  263.2 4.3 %broadcast_in_dim.22 = bf16[3,258,2,1536]{3,2,1,0:T(2,128)(2,1)} broadcast(bf16[3,258,1536]{2,1,0:T(8,128)(2,1)S(1)} %maximum_multiply_fusion), dimensions={0,1,3} | broadcast | bytes 7133184 | tf_op jit(solution)/shard_map/broadcast_in_dim | solution.py:62
  267.5 6.4 %reshape.42 = bf16[3,516,1536,1]{2,1,0,3:T(8,128)(2,1)} reshape(bf16[3,258,2,1536]{3,2,1,0:T(2,128)(2,1)} %broadcast_in_dim.22) | data formatting | bytes 9510912 | tf_op jit(solution)/shard_map/mul | solution.py:62
  273.9 14.4 %fusion.2 = f32[3,516,5,320]{3,1,2,0:T(8,128)S(1)} fusion(bf16[5,320,1536]{2,1,0:T(8,128)(2,1)} %param.7, bf16[3,516,1536,1]{2,1,0,3:T(8,128)(2,1)} %reshape.42), kind=kOutput, calls=%fused_computation.4 | convolution fusion | flops 7608729600 | bytes 19577856 | tf_op jit(solution)/shard_map/sqo,jo->sqj/dot_general | solution.py:63
  288.4 0.0 copy-done
  288.4 2.1 fusion.18
  290.5 1.4 copy.20
  291.9 1.0 copy.27
  292.9 0.7 convert_element_type.47
  293.6 8.8 %reduce-scatter.13.cloned.1.call-done = bf16[384,1600]{1,0:T(8,128)(2,1)} async-done(((bf16[1536,1600]{1,0:T(8,128)(2,1)}), bf16[384,1600]{1,0:T(8,128)(2,1)}) %reduce-scatter.13.cloned.1.call-update) | async-done | bytes 1228816
  302.4 3.3 %reshape.50 = bf16[384,5,320]{2,1,0:T(8,128)(2,1)S(1)} reshape(bf16[384,1600]{1,0:T(8,128)(2,1)} %reduce-scatter.13.cloned.1.call-done) | data formatting | bytes 2457600
  305.6 2.4 copy.25
  308.0 2.9 convert_element_type.45
  (9 shorter events, 0.0 us)
Async XLA Ops:
  7.2 59.0 %all-gather.3.cloned.1.call-start = ((), (), s32[]{:S(2)}) async-start(), calls=%async_computation.5 | async-start | bytes 1966080 | tf_op jit(solution)/shard_map/all_gather | solution.py:46
  8.9 9.8 %copy-start.3 = (s32[512]{0:T(512)S(1)}, s32[512]{0:T(512)}, u32[]{:S(2)}) copy-start(s32[512]{0:T(512)} %param.9) | copy-start | bytes 6148
  15.0 10.0 %collective-permute-start = (bf16[3,2,320]{2,1,0:T(2,128)(2,1)S(1)}, bf16[3,2,320]{2,1,0:T(2,128)(2,1)S(1)}, u32[]{:S(2)}, u32[]{:S(2)}) collective-permute-start(bf16[3,2,320]{2,1,0:T(2,128)(2,1)S(1)} %get-tuple-element.23), channel_id=1, source_target_pairs={{0,4},{4,8},{8,12},{1,5},{5,9},{9,13},{2,6},{6,10},{10,14},{3,7},{... | collective-permute-start | bytes 11528 | tf_op jit(solution)/shard_map/ppermute | solution.py:17
  17.4 7.6 %collective-permute-start.1 = (bf16[3,2,320]{2,1,0:T(2,128)(2,1)S(1)}, bf16[3,2,320]{2,1,0:T(2,128)(2,1)S(1)}, u32[]{:S(2)}, u32[]{:S(2)}) collective-permute-start(bf16[3,2,320]{2,1,0:T(2,128)(2,1)S(1)} %get-tuple-element.22), channel_id=1, source_target_pairs={{4,0},{8,4},{12,8},{5,1},{9,5},{13,9},{6,2},{10,6},{14,10},{7,3},{... | collective-permute-start | bytes 11528 | tf_op jit(solution)/shard_map/ppermute | solution.py:19
  24.9 90.7 %reduce-scatter.9.cloned.1.call-start = ((), (), s32[]{:S(2)}) async-start(), calls=%async_computation.4 | async-start | bytes 2949120 | tf_op jit(solution)/shard_map/reduce_scatter | solution.py:42
  62.8 0.7 copy-start.4
  62.8 52.8 %copy-start.2 = (s32[3,64,512]{2,1,0:T(8,128)S(1)}, s32[3,64,512]{2,1,0:T(8,128)}, u32[]{:S(2)}) copy-start(s32[3,64,512]{2,1,0:T(8,128)} %param.11) | copy-start | bytes 1179652
  62.8 84.5 %reduce-scatter.11.cloned.1.call-start = ((), (), s32[]{:S(2)}) async-start(), calls=%async_computation.7 | async-start | bytes 1966080 | tf_op jit(solution)/shard_map/reduce_scatter | solution.py:55
  115.6 2.3 copy-start.1
  119.7 79.6 %all-gather.5.cloned.1.call-start = ((), (), s32[]{:S(2)}) async-start(), calls=%async_computation.6 | async-start | bytes 2949120 | tf_op jit(solution)/shard_map/all_gather | solution.py:53
  122.5 169.4 %reduce-scatter.15.cloned.1.call-start = ((), (), s32[]{:S(2)}) async-start(), calls=%async_computation.9 | async-start | bytes 491520
  149.2 153.1 %reduce-scatter.13.cloned.1.call-start = ((), (), s32[]{:S(2)}) async-start(), calls=%async_computation.8 | async-start | bytes 6389760
  254.0 2.9 collective-permute-start.2
  255.5 4.5 %collective-permute-start.3 = (bf16[3,1,1536]{2,1,0:T(2,128)(2,1)S(1)}, bf16[3,1,1536]{2,1,0:T(2,128)(2,1)S(1)}, u32[]{:S(2)}, u32[]{:S(2)}) collective-permute-start(bf16[3,1,1536]{2,1,0:T(2,128)(2,1)S(1)} %get-tuple-element.15), channel_id=1, source_target_pairs={{4,0},{8,4},{12,8},{5,1},{9,5},{13,9},{6,2},{10,6},{14,10},{7,3},{... | collective-permute-start | bytes 27656 | tf_op jit(solution)/shard_map/ppermute | solution.py:19
  273.9 14.4 %copy-start = (f32[3,512,320]{2,1,0:T(8,128)S(1)}, f32[3,512,320]{2,1,0:T(8,128)}, u32[]{:S(2)}) copy-start(f32[3,512,320]{2,1,0:T(8,128)} %get-tuple-element.13) | copy-start | bytes 5898244
Sparse Core Ops, SparseCore 0:
  25.0 41.1 all-gather.2
  68.5 47.0 reduce-scatter.8
  119.8 27.4 reduce-scatter.10
  149.3 49.9 all-gather.4
  201.4 19.4 reduce-scatter.14
  253.1 49.2 reduce-scatter.12
where the time goes:
time: 320 us; the launch traced here: 318 us
  waiting for transfers between devices  131 us (41%)
  local copies, waits for them, and re-layouts  96.2 us (30%)
  matrix products  46.1 us (14%)
  other arithmetic  23.2 us (7%)
  between operations  14.3 us (4%)
  starting transfers between devices  6.99 us (2%)
    all_gather x1, waiting for transfers between devices, local(): slab_grad = lax.all_gather(grad_bins, 'chan', axis=1, tiled=True)  50 us
    reduce_scatter x1, waiting for transfers between devices, local(): lax.psum_scatter(pooled_part.astype(jnp.bfloat16), 'chan', scatter_dimens...  49.4 us
    unnamed x18, local copies, waits for them, and re-layouts  36.8 us
    reduce_scatter x1, waiting for transfers between devices, local(): lax.psum_scatter(track_part.astype(jnp.bfloat16), 'seq', scatter_dimensio...  16.8 us
    dot_general x1, matrix products, local(): jnp.einsum('sqo,jo->sqj', wide_grad, flat_weight, preferred_element_type=...  14.4 us
    dot_general x1, matrix products, local(): jnp.einsum('stj,sto->jo', windows, slab_upsampled, preferred_element_type...  12.5 us
    dot_general x1, matrix products, local(): jnp.einsum('stj,jo->sto', windows, flat_weight, preferred_element_type=jn...  12.4 us
    dot_general x1, local copies, waits for them, and re-layouts, local(): jnp.einsum('stj,jo->sto', windows, flat_weight, preferred_element_type=jn...  11 us
  transfers between devices with their start and end apart: 10, of which 6 were waited for; matrix products, arithmetic and copies ran while one was open for 46% of the time, Pallas kernels for 0%

commit v1 on v0

--- a/solution.py
+++ b/solution.py
@@ -4,6 +4,30 @@
 from jax.sharding import PartitionSpec as P
 
 KSIZE = 5
+
+
+def _detail_numbers(mat, out_dim):
+    item_now = list(mat.shape[1:])
+    item_now[out_dim] *= mat.shape[0]
+    return jnp.moveaxis(mat, 0, out_dim).reshape(item_now)
+
+
+def open_the_things(local_x, which_axis):
+    near = lax.axis_size(which_axis)
+    ready = lax.axis_index(which_axis)
+    tmp, piece_now = (near, ready)
+    lower, side_arr = (local_x[None], 1)
+    while side_arr < tmp:
+        tray = []
+        for w in [*range(tmp)]:
+            tray.append((w, w ^ side_arr))
+        now = lax.ppermute(lower, axis_name=which_axis, perm=tray)
+        latest = piece_now & side_arr == 0
+        then = jnp.where(latest, lower, now)
+        later = jnp.where(latest, now, lower)
+        lower = jnp.concatenate([then, later])
+        side_arr *= 2
+    return lower
 
 
 def padded_2(cells, sides, width):
@@ -50,7 +74,8 @@
     grad_bins = jnp.einsum(
         "snm,md->snd", grad_logit, chosen, preferred_element_type=jnp.float32
     ).astype(jnp.bfloat16)
-    slab_grad = lax.all_gather(grad_bins, "chan", axis=1, tiled=True)
+    block_out = open_the_things(grad_bins, "chan")
+    slab_grad = _detail_numbers(block_out, 1)
     track_part = jnp.einsum("snm,snd->md", grad_logit, bin_rows, preferred_element_type=jnp.float32)
     track_summed = lax.psum_scatter(
         track_part.astype(jnp.bfloat16), "seq", scatter_dimension=0, tiled=True

time: 320 us -> 310 us (0.969)
  waiting for transfers between devices: 131 us -> 120 us
  starting transfers between devices: 6.99 us -> 10.4 us
    ppermute x0 -> x2, waiting for transfers between devices: none -> 53.7 us  [open_the_things(): now = lax.ppermute(lower, axis_name=which_axis, perm=tray)]
    all_gather x1 -> x0, waiting for transfers between devices: 50 us -> none  [local(): slab_grad = lax.all_gather(grad_bins, 'chan', axis=1, tiled=True)]
    reduce_scatter x1, waiting for transfers between devices: 16.8 us -> 0.01 us  [local(): lax.psum_scatter(track_part.astype(jnp.bfloat16), 'seq', scatter_dimensio...]
    unnamed x8 -> x7, waiting for transfers between devices: 8.85 us -> 12.4 us
  transfers between devices with their start and end apart: 10 -> 11, of which waited for: 6 -> 6; matrix products, arithmetic and copies ran while one was open for 46% -> 46% of each run, Pallas kernels for 0% -> 0%
where the time goes in v1:
time: 310 us; the launch traced here: 308 us
  waiting for transfers between devices  120 us (39%)
  local copies, waits for them, and re-layouts  95.2 us (31%)
  matrix products  45.9 us (15%)
  other arithmetic  22.1 us (7%)
  between operations  14 us (5%)
  starting transfers between devices  10.4 us (3%)
    ppermute x2, waiting for transfers between devices, open_the_things(): now = lax.ppermute(lower, axis_name=which_axis, perm=tray)  53.7 us
    reduce_scatter x1, waiting for transfers between devices, local(): lax.psum_scatter(pooled_part.astype(jnp.bfloat16), 'chan', scatter_dimens...  49.4 us
    unnamed x18, local copies, waits for them, and re-layouts  36.8 us
    dot_general x1, matrix products, local(): jnp.einsum('sqo,jo->sqj', wide_grad, flat_weight, preferred_element_type=...  15.3 us
    dot_general x1, matrix products, local(): jnp.einsum('stj,sto->jo', windows, slab_upsampled, preferred_element_type...  12.6 us
    dot_general x1, matrix products, local(): jnp.einsum('stj,jo->sto', windows, flat_weight, preferred_element_type=jn...  12.4 us
    unnamed x7, waiting for transfers between devices  12.4 us
    dot_general x1, local copies, waits for them, and re-layouts, local(): jnp.einsum('stj,jo->sto', windows, flat_weight, preferred_element_type=jn...  10.9 us
  transfers between devices with their start and end apart: 11, of which 6 were waited for; matrix products, arithmetic and copies ran while one was open for 46% of the time, Pallas kernels for 0%

profile of v1, /device:TPU:0, one launch (start us, length us, event | category | flops | bytes accessed | tf_op | source)
XLA Modules:
  0.0 307.7 jit_solution(5509166491885590935)
XLA Ops:
  7.2 0.0 all-gather.2.cloned.1.call-start
  7.2 1.7 copy.18
  8.9 0.0 copy-start.3
  8.9 6.0 %fusion.13 = (bf16[3,512,320]{2,1,0:T(8,128)(2,1)S(1)}, f32[3,512,320]{2,1,0:T(8,128)}) fusion(bf16[3,512,320]{2,1,0:T(8,128)(2,1)S(1)} %copy.18), kind=kLoop, calls=%fused_computation.20 | loop fusion | flops 32440320 | bytes 3932160 | tf_op jit(solution)/shard_map/convert_element_type | solution.py:58
  15.0 1.3 collective-permute-start.1
  16.3 3.0 collective-permute-start
  19.3 5.2 %gather_fusion = bf16[512,384]{1,0:T(8,128)(2,1)S(1)} fusion(bf16[7611,384]{1,0:T(8,128)(2,1)} %param.8, s32[1024]{0:T(1024)S(1)} %pad_clamp_fusion), kind=kCustom, calls=%fused_computation | custom fusion | bytes 788480 | tf_op jit(solution)/shard_map/jit(_take)/gather | solution.py:69
  24.6 0.9 broadcast_select_fusion.4
  25.5 0.0 all-gather.2.cloned.1.call-update
  25.5 0.0 reduce-scatter.9.cloned.1.call-start
  25.5 0.0 collective-permute-done.1
  25.5 0.0 collective-permute-done
  25.6 3.4 %pad_maximum_fusion = (bf16[3,512,320]{2,1,0:T(8,128)(2,1)S(1)}, bf16[3,512,320]{2,1,0:T(8,128)(2,1)}, bf16[3,512,320]{2,1,0:T(8,128)(2,1)}, bf16[3,512,320]{2,1,0:T(8,128)(2,1)}) fusion(bf16[3,2,320]{2,1,0:T(2,128)(2,1)S(1)} %collective-permute-done.1, bf16[3,512,320]{2,1,0:T(8,128)(2,1)S(1)} %get-tuple-element.12, ...), kind=kLoop, calls=%fused_computation.73 | loop fusion | flops 7864320 | bytes 4922880 | tf_op jit(solution)/shard_map/concatenate | solution.py:39
  28.9 9.0 %concatenate.23 = bf16[3,512,1600]{2,1,0:T(8,128)(2,1)} concatenate(bf16[3,512,320]{2,1,0:T(8,128)(2,1)} %get-tuple-element.24, bf16[3,512,320]{2,1,0:T(8,128)(2,1)} %get-tuple-element.25, bf16[3,512,320]{2,1,0:T(8,128)(2,1)S(1)} %get-tuple-element.12, bf16[3,512,320]{2,1,0:T(8,128)(2,1)} %get-tuple-element.19, bf16[3,512,320]{2,1,0:T(8,128)(2,1)S(1)} %get-tuple-element.18), dimensions={2} | concatenate | bytes 9830400 | tf_op jit(solution)/shard_map/concatenate | solution.py:60
  37.9 10.9 %dot_general.24 = bf16[3,256,2,1600]{3,2,1,0:T(2,128)(2,1)} reshape(bf16[3,512,1600]{2,1,0:T(8,128)(2,1)} %concatenate.23) | data formatting | bytes 9830400 | tf_op jit(solution)/shard_map/stj,jo->sto/dot_general | solution.py:64
  48.8 12.4 %fusion.7 = f32[3,256,1536]{2,1,0:T(8,128)S(1)} fusion(bf16[1600,1536,1,1]{1,0,3,2:T(8,128)(2,1)} %bitcast.63, bf16[3,256,2,1600]{3,2,1,0:T(2,128)(2,1)} %dot_general.24), kind=kOutput, calls=%fused_computation.14 | convolution fusion | flops 7550926848 | bytes 14548992 | tf_op jit(solution)/shard_map/stj,jo->sto/dot_general | solution.py:64
  61.2 2.0 multiply_convert_fusion
  63.3 0.0 reduce-scatter.9.cloned.1.call-update
  63.3 0.0 reduce-scatter.11.cloned.1.call-start
  63.3 0.6 copy-done.4
  64.0 1.0 all-gather.2.cloned.1.call-done
  65.0 49.4 %reduce-scatter.9.cloned.1.call-done = bf16[3,64,1536]{2,1,0:T(8,128)(2,1)} async-done(((bf16[3,256,1536]{2,1,0:T(8,128)(2,1)}), bf16[3,64,1536]{2,1,0:T(8,128)(2,1)}) %reduce-scatter.9.cloned.1.call-update) | async-done | bytes 589840 | tf_op jit(solution)/shard_map/reduce_scatter | solution.py:66
  114.3 0.0 copy-done.2
  114.3 2.3 fusion.63
  116.6 0.5 fusion.12
  117.1 0.9 collective-permute-start.2
  118.0 2.8 fusion.6
  120.9 0.0 reduce-scatter.11.cloned.1.call-update
  120.9 0.2 reduce-scatter.15.cloned.1.call-start
  121.1 10.9 %collective-permute-done.2 = bf16[1,3,64,1536]{3,2,1,0:T(8,128)(2,1)} collective-permute-done((bf16[1,3,64,1536]{3,2,1,0:T(8,128)(2,1)S(1)}, bf16[1,3,64,1536]{3,2,1,0:T(8,128)(2,1)}, u32[]{:S(2)}, u32[]{:S(2)}) %collective-permute-start.2) | collective-permute-done | bytes 589856 | tf_op jit(solution)/shard_map/ppermute | solution.py:24
  132.0 1.1 broadcast_select_fusion.3
  133.1 0.1 pad_maximum_fusion.2
  133.2 2.2 collective-permute-start.3
  135.4 7.7 %copy.21 = bf16[1600,3,512]{2,0,1:T(8,128)(2,1)} copy(bf16[1600,3,512]{0,2,1:T(8,128)(2,1)} %bitcast.55) | data formatting | bytes 9830400 | tf_op jit(solution)/shard_map/stj,sto->jo/dot_general | solution.py:97
  143.2 42.9 %collective-permute-done.3 = bf16[2,3,64,1536]{3,2,1,0:T(8,128)(2,1)} collective-permute-done((bf16[2,3,64,1536]{3,2,1,0:T(8,128)(2,1)S(1)}, bf16[2,3,64,1536]{3,2,1,0:T(8,128)(2,1)}, u32[]{:S(2)}, u32[]{:S(2)}) %collective-permute-start.3) | collective-permute-done | bytes 1179680 | tf_op jit(solution)/shard_map/ppermute | solution.py:24
  186.0 1.4 broadcast_select_fusion.1
  187.5 0.2 maximum_bitcast_fusion
  187.7 0.2 copy.20
  187.8 0.4 broadcast_multiply_fusion
  188.2 4.0 %broadcast_in_dim.27 = bf16[3,256,2,1536]{3,2,1,0:T(2,128)(2,1)} broadcast(bf16[3,256,1536]{2,1,0:T(8,128)(2,1)S(1)} %broadcast_multiply_fusion), dimensions={0,1,3} | broadcast | bytes 7077888 | tf_op jit(solution)/shard_map/broadcast_in_dim | solution.py:96
  192.2 10.7 %reshape.48 = bf16[3,512,1536,1]{2,1,0,3:T(8,128)(2,1)} reshape(bf16[3,256,2,1536]{3,2,1,0:T(2,128)(2,1)} %broadcast_in_dim.27) | data formatting | bytes 9437184 | tf_op jit(solution)/shard_map/mul | solution.py:96
  202.9 1.9 copy.28
  204.8 0.0 reduce-scatter.15.cloned.1.call-update
  204.9 0.0 reduce-scatter.13.cloned.1.call-start
  204.9 12.6 %bitcast_convert_fusion = bf16[5,320,1536]{2,1,0:T(8,128)(2,1)} fusion(bf16[5,320,3,512]{3,1,0,2:T(8,128)(2,1)} %bitcast.60, bf16[3,512,1536,1]{2,1,0,3:T(8,128)(2,1)} %reshape.48), kind=kOutput, calls=%fused_computation.1 | convolution fusion | flops 7552204800 | bytes 14548992 | tf_op jit(solution)/shard_map/stj,sto->jo/dot_general | solution.py:97
  217.5 11.7 %copy.26 = bf16[5,320,1536]{1,0,2:T(8,128)(2,1)} copy(bf16[5,320,1536]{2,1,0:T(8,128)(2,1)} %bitcast_convert_fusion) | data formatting | bytes 9830400
  229.2 12.8 %reshape.53 = bf16[1536,1600]{1,0:T(8,128)(2,1)} reshape(bf16[1536,5,320]{2,1,0:T(8,128)(2,1)} %bitcast.56) | data formatting | bytes 9830400
  242.0 0.0 reduce-scatter.13.cloned.1.call-update
  242.1 1.3 collective-permute-start.4
  243.4 1.3 collective-permute-start.5
  244.7 0.0 collective-permute-done.4
  244.7 3.6 %collective-permute-done.5 = bf16[3,1,1536]{2,1,0:T(2,128)(2,1)S(1)} collective-permute-done((bf16[3,1,1536]{2,1,0:T(2,128)(2,1)S(1)}, bf16[3,1,1536]{2,1,0:T(2,128)(2,1)S(1)}, u32[]{:S(2)}, u32[]{:S(2)}) %collective-permute-start.5) | collective-permute-done | bytes 9248 | tf_op jit(solution)/shard_map/ppermute | solution.py:43
  248.2 0.8 maximum_multiply_fusion
  249.0 4.3 %broadcast_in_dim.26 = bf16[3,258,2,1536]{3,2,1,0:T(2,128)(2,1)} broadcast(bf16[3,258,1536]{2,1,0:T(8,128)(2,1)S(1)} %maximum_multiply_fusion), dimensions={0,1,3} | broadcast | bytes 7133184 | tf_op jit(solution)/shard_map/broadcast_in_dim | solution.py:87
  253.2 6.5 %reshape.46 = bf16[3,516,1536,1]{2,1,0,3:T(8,128)(2,1)} reshape(bf16[3,258,2,1536]{3,2,1,0:T(2,128)(2,1)} %broadcast_in_dim.26) | data formatting | bytes 9510912 | tf_op jit(solution)/shard_map/mul | solution.py:87
  259.7 15.3 %fusion.2 = f32[3,516,5,320]{3,1,2,0:T(8,128)S(1)} fusion(bf16[5,320,1536]{2,1,0:T(8,128)(2,1)} %param.7, bf16[3,516,1536,1]{2,1,0,3:T(8,128)(2,1)} %reshape.46), kind=kOutput, calls=%fused_computation.4 | convolution fusion | flops 7608729600 | bytes 19577856 | tf_op jit(solution)/shard_map/sqo,jo->sqj/dot_general | solution.py:88
  275.0 2.1 fusion.19
  277.2 1.4 copy.22
  278.5 1.0 copy.29
  279.6 0.7 convert_element_type.47
  280.3 12.3 %reduce-scatter.13.cloned.1.call-done = bf16[384,1600]{1,0:T(8,128)(2,1)} async-done(((bf16[1536,1600]{1,0:T(8,128)(2,1)}), bf16[384,1600]{1,0:T(8,128)(2,1)}) %reduce-scatter.13.cloned.1.call-update) | async-done | bytes 1228816
  292.6 3.3 %reshape.54 = bf16[384,5,320]{2,1,0:T(8,128)(2,1)S(1)} reshape(bf16[384,1600]{1,0:T(8,128)(2,1)} %reduce-scatter.13.cloned.1.call-done) | data formatting | bytes 2457600
  295.8 2.4 copy.27
  298.2 2.9 convert_element_type.45
  (15 shorter events, 0.1 us)
Async XLA Ops:
  7.2 57.8 %all-gather.2.cloned.1.call-start = ((), (), s32[]{:S(2)}) async-start(), calls=%async_computation.5 | async-start | bytes 1966080 | tf_op jit(solution)/shard_map/all_gather | solution.py:70
  8.9 10.4 %copy-start.3 = (s32[512]{0:T(512)S(1)}, s32[512]{0:T(512)}, u32[]{:S(2)}) copy-start(s32[512]{0:T(512)} %param.9) | copy-start | bytes 6148
  15.0 10.6 %collective-permute-start.1 = (bf16[3,2,320]{2,1,0:T(2,128)(2,1)S(1)}, bf16[3,2,320]{2,1,0:T(2,128)(2,1)S(1)}, u32[]{:S(2)}, u32[]{:S(2)}) collective-permute-start(bf16[3,2,320]{2,1,0:T(2,128)(2,1)S(1)} %get-tuple-element.26), channel_id=1, source_target_pairs={{4,0},{8,4},{12,8},{5,1},{9,5},{13,9},{6,2},{10,6},{14,10},{7,3},{... | collective-permute-start | bytes 11528 | tf_op jit(solution)/shard_map/ppermute | solution.py:43
  16.3 9.3 %collective-permute-start = (bf16[3,2,320]{2,1,0:T(2,128)(2,1)S(1)}, bf16[3,2,320]{2,1,0:T(2,128)(2,1)S(1)}, u32[]{:S(2)}, u32[]{:S(2)}) collective-permute-start(bf16[3,2,320]{2,1,0:T(2,128)(2,1)S(1)} %get-tuple-element.27), channel_id=1, source_target_pairs={{0,4},{4,8},{8,12},{1,5},{5,9},{9,13},{2,6},{6,10},{10,14},{3,7},{... | collective-permute-start | bytes 11528 | tf_op jit(solution)/shard_map/ppermute | solution.py:41
  25.5 88.8 %reduce-scatter.9.cloned.1.call-start = ((), (), s32[]{:S(2)}) async-start(), calls=%async_computation.4 | async-start | bytes 2949120 | tf_op jit(solution)/shard_map/reduce_scatter | solution.py:66
  63.3 0.7 copy-start.4
  63.3 51.1 %copy-start.2 = (s32[3,64,512]{2,1,0:T(8,128)S(1)}, s32[3,64,512]{2,1,0:T(8,128)}, u32[]{:S(2)}) copy-start(s32[3,64,512]{2,1,0:T(8,128)} %param.11) | copy-start | bytes 1179652
  63.3 139.6 %reduce-scatter.11.cloned.1.call-start = ((), (), s32[]{:S(2)}) async-start(), calls=%async_computation.6 | async-start | bytes 1966080 | tf_op jit(solution)/shard_map/reduce_scatter | solution.py:80
  65.0 51.7 %copy-start.1 = (bf16[512,1536]{1,0:T(8,128)(2,1)S(1)}, bf16[512,1536]{1,0:T(8,128)(2,1)}, u32[]{:S(2)}) copy-start(bf16[512,1536]{1,0:T(8,128)(2,1)} %all-gather.2.cloned.1.call-done) | copy-start | bytes 4718596
  117.1 14.9 %collective-permute-start.2 = (bf16[1,3,64,1536]{3,2,1,0:T(8,128)(2,1)S(1)}, bf16[1,3,64,1536]{3,2,1,0:T(8,128)(2,1)}, u32[]{:S(2)}, u32[]{:S(2)}) collective-permute-start(bf16[1,3,64,1536]{3,2,1,0:T(8,128)(2,1)S(1)} %fusion.12), channel_id=1, source_target_pairs={{0,1},{1,0},{2,3},{3,2},{4,5},{5,4},{6,7},{7,6},{8,9},{9,8},{10,11... | collective-permute-start | bytes 1769480 | tf_op jit(solution)/shard_map/ppermute | solution.py:24
  120.9 157.7 %reduce-scatter.15.cloned.1.call-start = ((), (), s32[]{:S(2)}) async-start(), calls=%async_computation.8 | async-start | bytes 491520
  133.2 52.8 %collective-permute-start.3 = (bf16[2,3,64,1536]{3,2,1,0:T(8,128)(2,1)S(1)}, bf16[2,3,64,1536]{3,2,1,0:T(8,128)(2,1)}, u32[]{:S(2)}, u32[]{:S(2)}) collective-permute-start(bf16[2,3,64,1536]{3,2,1,0:T(8,128)(2,1)S(1)} %pad_maximum_fusion.2), channel_id=1, source_target_pairs={{0,2},{1,3},{2,0},{3,1},{4,6},{5,7},{6,4},{7,5},{8,10},{9,11},{10,... | collective-permute-start | bytes 3538952 | tf_op jit(solution)/shard_map/ppermute | solution.py:24
  204.9 87.7 %reduce-scatter.13.cloned.1.call-start = ((), (), s32[]{:S(2)}) async-start(), calls=%async_computation.7 | async-start | bytes 6389760
  242.1 2.6 collective-permute-start.4
  243.4 4.9 %collective-permute-start.5 = (bf16[3,1,1536]{2,1,0:T(2,128)(2,1)S(1)}, bf16[3,1,1536]{2,1,0:T(2,128)(2,1)S(1)}, u32[]{:S(2)}, u32[]{:S(2)}) collective-permute-start(bf16[3,1,1536]{2,1,0:T(2,128)(2,1)S(1)} %get-tuple-element.15), channel_id=1, source_target_pairs={{4,0},{8,4},{12,8},{5,1},{9,5},{13,9},{6,2},{10,6},{14,10},{7,3},{... | collective-permute-start | bytes 27656 | tf_op jit(solution)/shard_map/ppermute | solution.py:43
  259.7 15.3 %copy-start = (f32[3,512,320]{2,1,0:T(8,128)S(1)}, f32[3,512,320]{2,1,0:T(8,128)}, u32[]{:S(2)}) copy-start(f32[3,512,320]{2,1,0:T(8,128)} %get-tuple-element.13) | copy-start | bytes 5898244
Sparse Core Ops, SparseCore 0:
  25.6 39.3 all-gather.1
  67.3 47.0 reduce-scatter.8
  121.0 28.0 reduce-scatter.10
  205.0 20.6 reduce-scatter.14
  242.1 50.3 reduce-scatter.12
